TPU v7x, 32 devices: a whole 2x2x4 slice. The times are simulated.
32 devices in a mesh: node: 4 (over z), dom: 8 (over y, x, core).
Axes of the slice: x: 2, y: 2, z: 4, core: 2. Of those that a mesh axis runs over, the one named last changes fastest.
Arguments:
- probes: float32 [32, 16, 16, 128], P(None, 'dom'), may hold values from -24 to 24
- slope: float32 [16, 16, 128], P('dom'), may hold values from 4 to 6
- root: float32 [16, 16, 128], P('dom'), may hold values from 0.3 to 0.7
- damping: float32 [16, 16, 128], P('dom'), may hold values from 0.3 to 1.2
Outputs:
- moments: float32 [2, 2, 32, 16, 16, 128], P(None, None, 'node', 'dom')
- projections: float32 [2, 2, 32, 32], replicated
All inputs are finite; a program needn't handle non-finite values.
Results may differ from a plain program's by a relative error of at most 0.00013.
Values sent between devices are 32-bit elements; how exact they have to be, the bound alone decides.
A program may use at most 64 MiB of HBM per device.

v0:
```python
import math
import jax
import jax.numpy as jnp
from jax import lax
from jax.sharding import PartitionSpec as P

NODE_DEV = 2
SWEEPS = 8
CENTRE = 0.5
RADIUS = 2.0


def grid_step(source, fields, factor_re, factor_im):
    padded = jnp.pad(fields, ((0, 0), (0, 0), (1, 1), (1, 1), (1, 1)))
    total = padded[:, :, 2:, 1:-1, 1:-1] + padded[:, :, :-2, 1:-1, 1:-1]
    total = total + padded[:, :, 1:-1, 2:, 1:-1] + padded[:, :, 1:-1, :-2, 1:-1]
    total = total + padded[:, :, 1:-1, 1:-1, 2:] + padded[:, :, 1:-1, 1:-1, :-2]
    real_part = source + total[:, 0]
    imag_part = total[:, 1]
    return jnp.stack(
        [
            real_part * factor_re - imag_part * factor_im,
            real_part * factor_im + imag_part * factor_re,
        ],
        axis=1,
    )


def inverse_diagonal(shift_real, shift_imaginary, slope, root, damping, guard):
    zr_col = shift_real[:, None, None, None, None]
    zi_col = shift_imaginary[:, None, None, None, None]
    decay = jnp.exp(-zr_col)
    real_d = slope * (zr_col - root) + damping * (decay * jnp.cos(zi_col))
    imag_d = slope * zi_col - damping * (decay * jnp.sin(zi_col))
    scale = 1.0 / (real_d * real_d + imag_d * imag_d + guard)
    return (real_d * scale, -imag_d * scale)


def per_system(fields, weight_re, weight_im):
    a_col = weight_re[:, None, None, None]
    b_col = weight_im[:, None, None, None]
    return jnp.stack(
        [a_col * fields[:, 0] - b_col * fields[:, 1], a_col * fields[:, 1] + b_col * fields[:, 0]]
    )


def body(probes, slope, root, damping):
    vectors = probes.shape[0]
    planes = probes.shape[1]
    groups = lax.axis_size("node")
    total = NODE_DEV * groups
    first = (lax.axis_index("node") * NODE_DEV).astype(jnp.float32)
    dom_size = lax.axis_size("dom")
    count = NODE_DEV * vectors // dom_size
    replicated = jnp.broadcast_to(probes[None], (NODE_DEV,) + probes.shape).reshape(
        (NODE_DEV * vectors,) + probes.shape[1:]
    )
    own = lax.all_to_all(replicated, "dom", split_axis=0, concat_axis=1, tiled=True)
    slope_all, root_all, damping_all = (
        lax.all_gather(slope, "dom", axis=0, tiled=True),
        lax.all_gather(root, "dom", axis=0, tiled=True),
        lax.all_gather(damping, "dom", axis=0, tiled=True),
    )
    system = lax.axis_index("dom") * count + jnp.arange(count)
    position = first + (system // vectors).astype(jnp.float32)
    theta = 2.0 * math.pi * (position + 0.5) / total
    shift_real = CENTRE + RADIUS * jnp.cos(theta)
    shift_imaginary = RADIUS * jnp.sin(theta)
    qre, qim = inverse_diagonal(
        shift_real, shift_imaginary, slope_all[None], root_all[None], damping_all[None], 0.0
    )
    qre = qre[:, 0]
    qim = qim[:, 0]
    fields = jnp.stack([own * qre, own * qim], axis=1)
    for sweep in range(SWEEPS):
        fields = grid_step(own, fields, qre, qim)
    weight_re = RADIUS * jnp.cos(theta) / total
    weight_im = RADIUS * jnp.sin(theta) / total
    shifted_re = weight_re * shift_real - weight_im * shift_imaginary
    shifted_im = weight_re * shift_imaginary + weight_im * shift_real
    terms = jnp.stack(
        [per_system(fields, weight_re, weight_im), per_system(fields, shifted_re, shifted_im)]
    )
    back = lax.all_to_all(terms, "dom", split_axis=3, concat_axis=2, tiled=True)
    local = jnp.sum(back.reshape((2, 2, NODE_DEV, vectors) + probes.shape[1:]), axis=2)
    flat = local.reshape(4 * vectors, -1)
    basis = probes.reshape(vectors, -1)
    partial_value = lax.dot_general(
        flat,
        basis,
        (((1,), (1,)), ((), ())),
        precision=lax.Precision.HIGHEST,
        preferred_element_type=jnp.float32,
    )
    cells = planes * probes.shape[2] * probes.shape[3] * lax.axis_size("dom")
    projections = lax.psum(partial_value.reshape(2, 2, vectors, vectors) / cells, ("node", "dom"))
    summed = lax.psum(local, "node")
    share = vectors // groups
    moments = lax.dynamic_slice_in_dim(summed, lax.axis_index("node") * share, share, 2)
    return (moments, projections)


def solution(mesh):
    in_specs = (
        P(None, "dom", None, None),
        P("dom", None, None),
        P("dom", None, None),
        P("dom", None, None),
    )
    out_specs = (P(None, None, "node", "dom", None, None), P())
    return jax.shard_map(body, mesh=mesh, in_specs=in_specs, out_specs=out_specs, check_vma=False)
```

profile of v0, /device:TPU:0, one launch (start us, length us, event | category | flops | bytes accessed | tf_op | source)
XLA Modules:
  0.0 260.8 jit_solution(6893673430703613702)
XLA Ops:
  7.2 2.2 broadcast_in_dim.2
  9.4 5.2 %all-to-all-start = ((f32[64,2,16,128]{3,2,1,0:T(8,128)}), f32[64,2,16,128]{3,2,1,0:T(8,128)S(1)}, u32[]{:S(2)}, u32[]{:S(2)}) async-start(f32[64,2,16,128]{3,2,1,0:T(8,128)} %bitcast), calls=%async_computation | async-start | bytes 2097152 | tf_op jit(solution)/shard_map/all_to_all | solution.py:58
  14.6 18.8 %all_gather.9 = f32[16,16,128]{2,1,0:T(8,128)S(1)} all-gather(f32[2,16,128]{2,1,0:T(8,128)S(1)} %copy-done.2), channel_id=1, replica_groups=mesh['node'=4,'dom'=8] {'dom'}, dimensions={0}, use_global_device_ids=true | all-gather | bytes 147456 | tf_op jit(solution)/shard_map/all_gather | solution.py:60
  33.4 8.3 %all_gather.10 = f32[16,16,128]{2,1,0:T(8,128)S(1)} all-gather(f32[2,16,128]{2,1,0:T(8,128)S(1)} %copy-done.3), channel_id=1, replica_groups=mesh['node'=4,'dom'=8] {'dom'}, dimensions={0}, use_global_device_ids=true | all-gather | bytes 147456 | tf_op jit(solution)/shard_map/all_gather | solution.py:61
  41.7 9.1 %all_gather.11 = f32[16,16,128]{2,1,0:T(8,128)S(1)} all-gather(f32[2,16,128]{2,1,0:T(8,128)S(1)} %copy-done.4), channel_id=1, replica_groups=mesh['node'=4,'dom'=8] {'dom'}, dimensions={0}, use_global_device_ids=true | all-gather | bytes 147456 | tf_op jit(solution)/shard_map/all_gather | solution.py:62
  50.8 0.1 multiply_subtract_fusion.12
  50.9 0.0 all-to-all-done
  50.9 0.1 copy.15
  51.0 0.6 fusion.19
  51.6 2.6 select_maximum_fusion.7
  54.2 3.3 %slice_add_fusion.35 = f32[8,2,16,16,128]{4,3,2,0,1:T(8,128)S(1)} fusion(f32[8,2,18,18,130]{4,3,2,0,1:T(8,128)S(1)} %select_maximum_fusion.7), kind=kLoop, calls=%fused_computation.56 | loop fusion | flops 2621440 | bytes 14680064 | tf_op jit(solution)/shard_map/add | solution.py:17
  57.5 0.8 multiply_subtract_fusion.10
  58.3 2.4 select_maximum_fusion.6
  60.7 3.3 %slice_add_fusion.30 = f32[8,2,16,16,128]{4,3,2,0,1:T(8,128)S(1)} fusion(f32[8,2,18,18,130]{4,3,2,0,1:T(8,128)S(1)} %select_maximum_fusion.6), kind=kLoop, calls=%fused_computation.51 | loop fusion | flops 2621440 | bytes 14680064 | tf_op jit(solution)/shard_map/add | solution.py:17
  63.9 0.8 multiply_subtract_fusion.9
  64.7 2.4 select_maximum_fusion.5
  67.1 3.3 %slice_add_fusion.25 = f32[8,2,16,16,128]{4,3,2,0,1:T(8,128)S(1)} fusion(f32[8,2,18,18,130]{4,3,2,0,1:T(8,128)S(1)} %select_maximum_fusion.5), kind=kLoop, calls=%fused_computation.46 | loop fusion | flops 2621440 | bytes 14680064 | tf_op jit(solution)/shard_map/add | solution.py:17
  70.4 0.8 multiply_subtract_fusion.8
  71.2 2.4 select_maximum_fusion.4
  73.6 3.3 %slice_add_fusion.20 = f32[8,2,16,16,128]{4,3,2,0,1:T(8,128)S(1)} fusion(f32[8,2,18,18,130]{4,3,2,0,1:T(8,128)S(1)} %select_maximum_fusion.4), kind=kLoop, calls=%fused_computation.41 | loop fusion | flops 2621440 | bytes 14680064 | tf_op jit(solution)/shard_map/add | solution.py:17
  76.8 0.8 multiply_subtract_fusion.7
  77.6 2.6 select_maximum_fusion.3
  80.2 3.3 %slice_add_fusion.15 = f32[8,2,16,16,128]{4,3,2,0,1:T(8,128)S(1)} fusion(f32[8,2,18,18,130]{4,3,2,0,1:T(8,128)S(1)} %select_maximum_fusion.3), kind=kLoop, calls=%fused_computation.36 | loop fusion | flops 2621440 | bytes 14680064 | tf_op jit(solution)/shard_map/add | solution.py:17
  83.5 0.8 multiply_subtract_fusion.6
  84.3 2.4 select_maximum_fusion.2
  86.7 3.3 %slice_add_fusion.10 = f32[8,2,16,16,128]{4,3,2,0,1:T(8,128)S(1)} fusion(f32[8,2,18,18,130]{4,3,2,0,1:T(8,128)S(1)} %select_maximum_fusion.2), kind=kLoop, calls=%fused_computation.31 | loop fusion | flops 2621440 | bytes 14680064 | tf_op jit(solution)/shard_map/add | solution.py:17
  90.0 0.8 multiply_subtract_fusion.5
  90.8 2.4 select_maximum_fusion.1
  93.1 3.3 %slice_add_fusion.5 = f32[8,2,16,16,128]{4,3,2,0,1:T(8,128)S(1)} fusion(f32[8,2,18,18,130]{4,3,2,0,1:T(8,128)S(1)} %select_maximum_fusion.1), kind=kLoop, calls=%fused_computation.26 | loop fusion | flops 2621440 | bytes 14680064 | tf_op jit(solution)/shard_map/add | solution.py:17
  96.4 0.8 multiply_subtract_fusion.4
  97.2 2.4 select_maximum_fusion
  99.6 3.5 %slice_add_fusion = f32[8,2,16,16,128]{4,3,2,0,1:T(8,128)S(1)} fusion(f32[8,2,18,18,130]{4,3,2,0,1:T(8,128)S(1)} %select_maximum_fusion), kind=kLoop, calls=%fused_computation.21 | loop fusion | flops 2621440 | bytes 14680064 | tf_op jit(solution)/shard_map/add | solution.py:17
  103.1 0.9 multiply_subtract_fusion.1
  104.1 0.5 multiply_subtract_fusion
  104.6 0.4 maximum_bitcast_fusion
  105.0 0.4 pad_maximum_fusion
  105.4 0.6 copy.17
  106.0 51.6 %all_to_all.36 = f32[2,2,8,16,16,128]{5,4,2,1,0,3:T(8,128)S(1)} all-to-all(f32[2,2,8,16,16,128]{5,4,2,1,0,3:T(8,128)S(1)} %copy.17), channel_id=1, replica_groups=mesh['node'=4,'dom'=8] {'dom'}, dimensions={3} | all-to-all | bytes 8388608 | tf_op jit(solution)/shard_map/all_to_all | solution.py:84
  157.6 0.5 copy.19
  158.2 0.0 copy-start.1
  158.2 0.5 bitcast_reduce_fusion
  158.7 0.5 copy-done.1
  159.2 3.1 %fusion.10 = f32[2,2,32,32]{3,2,1,0:T(8,128)S(1)} fusion(f32[2,2,32,2,16,128]{5,4,3,2,1,0:T(8,128)S(1)} %bitcast_reduce_fusion, f32[32,2,16,128,1,1]{3,2,1,0,5,4:T(8,128)S(1)} %bitcast.53), kind=kOutput, calls=%fused_computation.66 | convolution fusion | flops 201330688 | bytes 2637824 | tf_op jit(solution)/shard_map/dot_general | solution.py:88
  162.3 0.0 all-reduce.10.cloned.1.call-start
  162.4 0.7 all-reduce.10.cloned.1.call-update
  163.1 42.9 %psum.15 = f32[2,2,32,32]{3,2,1,0:T(8,128)} all-reduce(f32[2,2,32,32]{3,2,1,0:T(8,128)S(1)} %fusion.10), channel_id=1, replica_groups=mesh['node'=4,'dom'=8] {'node','dom'}, use_global_device_ids=true, to_apply=%region_2.3 | all-reduce | flops 4096 | bytes 32768 | tf_op jit(solution)/shard_map/psum | solution.py:96
  206.0 46.1 %all-reduce.10.cloned.1.call-done = f32[2,2,32,2,16,128]{5,4,3,2,1,0:T(8,128)} async-done(((f32[2,2,32,2,16,128]{5,4,3,2,1,0:T(8,128)}), f32[2,2,32,2,16,128]{5,4,3,2,1,0:T(8,128)}) %all-reduce.10.cloned.1.call-update) | async-done | bytes 2097168 | tf_op jit(solution)/shard_map/psum | solution.py:97
  252.1 1.9 constant_dynamic-slice_fusion
  (9 shorter events, 0.1 us)
Async XLA Ops:
  7.2 7.4 %copy-start.2 = (f32[2,16,128]{2,1,0:T(8,128)S(1)}, f32[2,16,128]{2,1,0:T(8,128)}, u32[]{:S(2)}) copy-start(f32[2,16,128]{2,1,0:T(8,128)} %param.5) | copy-start | bytes 49156
  7.2 26.2 %copy-start.3 = (f32[2,16,128]{2,1,0:T(8,128)S(1)}, f32[2,16,128]{2,1,0:T(8,128)}, u32[]{:S(2)}) copy-start(f32[2,16,128]{2,1,0:T(8,128)} %param.6) | copy-start | bytes 49156
  7.2 34.5 %copy-start.4 = (f32[2,16,128]{2,1,0:T(8,128)S(1)}, f32[2,16,128]{2,1,0:T(8,128)}, u32[]{:S(2)}) copy-start(f32[2,16,128]{2,1,0:T(8,128)} %param.7) | copy-start | bytes 49156
  9.4 41.5 %all-to-all-start = ((f32[64,2,16,128]{3,2,1,0:T(8,128)}), f32[64,2,16,128]{3,2,1,0:T(8,128)S(1)}, u32[]{:S(2)}, u32[]{:S(2)}) async-start(f32[64,2,16,128]{3,2,1,0:T(8,128)} %bitcast), calls=%async_computation | async-start | bytes 2097152 | tf_op jit(solution)/shard_map/all_to_all | solution.py:58
  158.2 1.0 copy-start.1
  158.7 3.6 %copy-start = (f32[2,2,32,2,16,128]{5,4,3,2,1,0:T(8,128)}, f32[2,2,32,2,16,128]{5,4,3,2,1,0:T(8,128)S(1)}, u32[]{:S(2)}) copy-start(f32[2,2,32,2,16,128]{5,4,3,2,1,0:T(8,128)S(1)} %bitcast_reduce_fusion) | copy-start | bytes 6291460
  162.3 89.8 %all-reduce.10.cloned.1.call-start = ((), (), s32[]{:S(2)}) async-start(), calls=%async_computation.2 | async-start | bytes 4194304 | tf_op jit(solution)/shard_map/psum | solution.py:97
Sparse Core Ops, SparseCore 0:
  165.5 86.5 all-reduce.9
where the time goes:
time: 261 us
  blocking collectives  131 us (50%)
  other arithmetic  54.8 us (21%)
  waiting for transfers between devices  46.8 us (18%)
  between operations  14.3 us (5%)
  local copies, waits for them, and re-layouts  5.8 us (2%)
  starting transfers between devices  5.24 us (2%)
  matrix products  3.08 us (1%)
    all_to_all x1, blocking collectives, body(): back = lax.all_to_all(terms, 'dom', split_axis=3, concat_axis=2, tiled=True)  51.6 us
    psum x1, waiting for transfers between devices, body(): summed = lax.psum(local, 'node')  46.1 us
    psum x1, blocking collectives, body(): lax.psum(partial_value.reshape(2, 2, vectors, vectors) / cells, ('node',...  42.9 us
    add x8, other arithmetic, grid_step(): total = total + padded[:, :, 1:-1, 1:-1, 2:] + padded[:, :, 1:-1, 1:-1, :-2]  26.4 us
    all_gather x1, blocking collectives, body(): lax.all_gather(slope, 'dom', axis=0, tiled=True)  18.8 us
    another operation x7, other arithmetic, grid_step(): jnp.stack([real_part * factor_re - imag_part * factor_im, real_part * fac...  16.9 us
    all_gather x1, blocking collectives, body(): lax.all_gather(damping, 'dom', axis=0, tiled=True)  9.1 us
    all_gather x1, blocking collectives, body(): lax.all_gather(root, 'dom', axis=0, tiled=True)  8.31 us
  transfers between devices with their start and end apart: 2, of which 1 were waited for; matrix products, arithmetic and copies ran while one was open for 0% of the time, Pallas kernels for 0%

commit v1 on v0

--- a/solution.py
+++ b/solution.py
@@ -3,6 +3,7 @@
 import jax.numpy as jnp
 from jax import lax
 from jax.sharding import PartitionSpec as P
+from jax.lax import all_gather
 
 NODE_DEV = 2
 SWEEPS = 8
@@ -94,7 +95,7 @@
     )
     cells = planes * probes.shape[2] * probes.shape[3] * lax.axis_size("dom")
     projections = lax.psum(partial_value.reshape(2, 2, vectors, vectors) / cells, ("node", "dom"))
-    summed = lax.psum(local, "node")
+    summed = jnp.sum(all_gather(local, "node"), 0)
     share = vectors // groups
     moments = lax.dynamic_slice_in_dim(summed, lax.axis_index("node") * share, share, 2)
     return (moments, projections)

time: 261 us -> 323 us (1.24)
  waiting for transfers between devices: 46.8 us -> 96.1 us
  other arithmetic: 54.8 us -> 60.9 us
  blocking collectives: 131 us -> 137 us
    all_gather x0 -> x1, waiting for transfers between devices: none -> 96.1 us  [body(): summed = jnp.sum(all_gather(local, 'node'), 0)]
    psum x1 -> x0, waiting for transfers between devices: 46.1 us -> none  [body(): summed = lax.psum(local, 'node')]
    psum x1, blocking collectives: 42.9 us -> 49.5 us  [body(): lax.psum(partial_value.reshape(2, 2, vectors, vectors) / cells, ('node',...]
    reduce_sum x0 -> x1, other arithmetic: none -> 4.64 us  [body(): summed = jnp.sum(all_gather(local, 'node'), 0)]
  transfers between devices with their start and end apart: 2 -> 2, of which waited for: 1 -> 1; matrix products, arithmetic and copies ran while one was open for 0% -> 1% of each run, Pallas kernels for 0% -> 0%
where the time goes in v1:
time: 323 us
  blocking collectives  137 us (42%)
  waiting for transfers between devices  96.1 us (30%)
  other arithmetic  60.9 us (19%)
  between operations  14.3 us (4%)
  local copies, waits for them, and re-layouts  5.8 us (2%)
  starting transfers between devices  5.24 us (2%)
    all_gather x1, waiting for transfers between devices, body(): summed = jnp.sum(all_gather(local, 'node'), 0)  96.1 us
    all_to_all x1, blocking collectives, body(): back = lax.all_to_all(terms, 'dom', split_axis=3, concat_axis=2, tiled=True)  51.6 us
    psum x1, blocking collectives, body(): lax.psum(partial_value.reshape(2, 2, vectors, vectors) / cells, ('node',...  49.5 us
    add x8, other arithmetic, grid_step(): total = total + padded[:, :, 1:-1, 1:-1, 2:] + padded[:, :, 1:-1, 1:-1, :-2]  26.4 us
    all_gather x1, blocking collectives, body(): lax.all_gather(slope, 'dom', axis=0, tiled=True)  18.8 us
    another operation x7, other arithmetic, grid_step(): jnp.stack([real_part * factor_re - imag_part * factor_im, real_part * fac...  16.9 us
    all_gather x1, blocking collectives, body(): lax.all_gather(damping, 'dom', axis=0, tiled=True)  9.1 us
    all_gather x1, blocking collectives, body(): lax.all_gather(root, 'dom', axis=0, tiled=True)  8.31 us
  transfers between devices with their start and end apart: 2, of which 1 were waited for; matrix products, arithmetic and copies ran while one was open for 1% of the time, Pallas kernels for 0%

profile of v1, /device:TPU:0, one launch (start us, length us, event | category | flops | bytes accessed | tf_op | source)
XLA Modules:
  0.0 322.7 jit_solution(3880006488031442775)
XLA Ops:
  7.2 2.2 broadcast_in_dim.2
  9.4 5.2 %all-to-all-start = ((f32[64,2,16,128]{3,2,1,0:T(8,128)}), f32[64,2,16,128]{3,2,1,0:T(8,128)S(1)}, u32[]{:S(2)}, u32[]{:S(2)}) async-start(f32[64,2,16,128]{3,2,1,0:T(8,128)} %bitcast), calls=%async_computation | async-start | bytes 2097152 | tf_op jit(solution)/shard_map/all_to_all | solution.py:59
  14.6 0.0 all-gather.3.cloned.1.call-start
  14.6 18.8 %all_gather.15 = f32[16,16,128]{2,1,0:T(8,128)S(1)} all-gather(f32[2,16,128]{2,1,0:T(8,128)S(1)} %copy-done.2), channel_id=1, replica_groups=mesh['node'=4,'dom'=8] {'dom'}, dimensions={0}, use_global_device_ids=true | all-gather | bytes 147456 | tf_op jit(solution)/shard_map/all_gather | solution.py:61
  33.4 8.3 %all_gather.16 = f32[16,16,128]{2,1,0:T(8,128)S(1)} all-gather(f32[2,16,128]{2,1,0:T(8,128)S(1)} %copy-done.3), channel_id=1, replica_groups=mesh['node'=4,'dom'=8] {'dom'}, dimensions={0}, use_global_device_ids=true | all-gather | bytes 147456 | tf_op jit(solution)/shard_map/all_gather | solution.py:62
  41.7 9.1 %all_gather.17 = f32[16,16,128]{2,1,0:T(8,128)S(1)} all-gather(f32[2,16,128]{2,1,0:T(8,128)S(1)} %copy-done.4), channel_id=1, replica_groups=mesh['node'=4,'dom'=8] {'dom'}, dimensions={0}, use_global_device_ids=true | all-gather | bytes 147456 | tf_op jit(solution)/shard_map/all_gather | solution.py:63
  50.8 0.1 multiply_subtract_fusion.12
  50.9 0.1 copy.12
  51.0 0.6 fusion.19
  51.6 2.6 select_maximum_fusion.7
  54.2 3.3 %slice_add_fusion.35 = f32[8,2,16,16,128]{4,3,2,0,1:T(8,128)S(1)} fusion(f32[8,2,18,18,130]{4,3,2,0,1:T(8,128)S(1)} %select_maximum_fusion.7), kind=kLoop, calls=%fused_computation.56 | loop fusion | flops 2621440 | bytes 14680064 | tf_op jit(solution)/shard_map/add | solution.py:18
  57.5 0.8 multiply_subtract_fusion.10
  58.3 2.4 select_maximum_fusion.6
  60.7 3.3 %slice_add_fusion.30 = f32[8,2,16,16,128]{4,3,2,0,1:T(8,128)S(1)} fusion(f32[8,2,18,18,130]{4,3,2,0,1:T(8,128)S(1)} %select_maximum_fusion.6), kind=kLoop, calls=%fused_computation.51 | loop fusion | flops 2621440 | bytes 14680064 | tf_op jit(solution)/shard_map/add | solution.py:18
  63.9 0.8 multiply_subtract_fusion.9
  64.7 2.4 select_maximum_fusion.5
  67.1 3.3 %slice_add_fusion.25 = f32[8,2,16,16,128]{4,3,2,0,1:T(8,128)S(1)} fusion(f32[8,2,18,18,130]{4,3,2,0,1:T(8,128)S(1)} %select_maximum_fusion.5), kind=kLoop, calls=%fused_computation.46 | loop fusion | flops 2621440 | bytes 14680064 | tf_op jit(solution)/shard_map/add | solution.py:18
  70.4 0.8 multiply_subtract_fusion.8
  71.2 2.4 select_maximum_fusion.4
  73.6 3.3 %slice_add_fusion.20 = f32[8,2,16,16,128]{4,3,2,0,1:T(8,128)S(1)} fusion(f32[8,2,18,18,130]{4,3,2,0,1:T(8,128)S(1)} %select_maximum_fusion.4), kind=kLoop, calls=%fused_computation.41 | loop fusion | flops 2621440 | bytes 14680064 | tf_op jit(solution)/shard_map/add | solution.py:18
  76.8 0.8 multiply_subtract_fusion.7
  77.6 2.6 select_maximum_fusion.3
  80.2 3.3 %slice_add_fusion.15 = f32[8,2,16,16,128]{4,3,2,0,1:T(8,128)S(1)} fusion(f32[8,2,18,18,130]{4,3,2,0,1:T(8,128)S(1)} %select_maximum_fusion.3), kind=kLoop, calls=%fused_computation.36 | loop fusion | flops 2621440 | bytes 14680064 | tf_op jit(solution)/shard_map/add | solution.py:18
  83.5 0.8 multiply_subtract_fusion.6
  84.3 2.4 select_maximum_fusion.2
  86.7 3.3 %slice_add_fusion.10 = f32[8,2,16,16,128]{4,3,2,0,1:T(8,128)S(1)} fusion(f32[8,2,18,18,130]{4,3,2,0,1:T(8,128)S(1)} %select_maximum_fusion.2), kind=kLoop, calls=%fused_computation.31 | loop fusion | flops 2621440 | bytes 14680064 | tf_op jit(solution)/shard_map/add | solution.py:18
  90.0 0.8 multiply_subtract_fusion.5
  90.7 2.4 select_maximum_fusion.1
  93.1 3.3 %slice_add_fusion.5 = f32[8,2,16,16,128]{4,3,2,0,1:T(8,128)S(1)} fusion(f32[8,2,18,18,130]{4,3,2,0,1:T(8,128)S(1)} %select_maximum_fusion.1), kind=kLoop, calls=%fused_computation.26 | loop fusion | flops 2621440 | bytes 14680064 | tf_op jit(solution)/shard_map/add | solution.py:18
  96.4 0.8 multiply_subtract_fusion.4
  97.2 2.4 select_maximum_fusion
  99.6 3.5 %slice_add_fusion = f32[8,2,16,16,128]{4,3,2,0,1:T(8,128)S(1)} fusion(f32[8,2,18,18,130]{4,3,2,0,1:T(8,128)S(1)} %select_maximum_fusion), kind=kLoop, calls=%fused_computation.21 | loop fusion | flops 2621440 | bytes 14680064 | tf_op jit(solution)/shard_map/add | solution.py:18
  103.1 0.9 multiply_subtract_fusion.1
  104.1 0.5 multiply_subtract_fusion
  104.5 0.4 maximum_bitcast_fusion
  105.0 0.4 pad_maximum_fusion
  105.5 0.6 copy.14
  106.1 51.6 %all_to_all.36 = f32[2,2,8,16,16,128]{5,4,2,1,0,3:T(8,128)S(1)} all-to-all(f32[2,2,8,16,16,128]{5,4,2,1,0,3:T(8,128)S(1)} %copy.14), channel_id=1, replica_groups=mesh['node'=4,'dom'=8] {'dom'}, dimensions={3} | all-to-all | bytes 8388608 | tf_op jit(solution)/shard_map/all_to_all | solution.py:85
  157.6 0.5 copy.16
  158.2 0.0 copy-start.1
  158.2 1.9 bitcast_reduce_fusion
  160.1 0.0 all-gather.3.cloned.1.call-update
  160.2 1.6 copy-done
  161.7 3.1 fusion.10
  164.8 49.5 %psum.7 = f32[2,2,32,32]{3,2,1,0:T(8,128)} all-reduce(f32[2,2,32,32]{3,2,1,0:T(8,128)S(1)} %fusion.10), channel_id=1, replica_groups=mesh['node'=4,'dom'=8] {'node','dom'}, use_global_device_ids=true, to_apply=%region_2.3 | all-reduce | flops 4096 | bytes 32768 | tf_op jit(solution)/shard_map/psum | solution.py:97
  214.3 96.1 %all-gather.3.cloned.1.call-done = f32[8,2,32,2,16,128]{5,4,3,2,1,0:T(8,128)} async-done(((f32[2,2,32,2,16,128]{5,4,3,2,1,0:T(8,128)}), f32[8,2,32,2,16,128]{5,4,3,2,1,0:T(8,128)}) %all-gather.3.cloned.1.call-update) | async-done | bytes 8388624 | tf_op jit(solution)/shard_map/all_gather | solution.py:98
  310.3 4.6 %reduce_sum.19 = f32[2,2,32,2,16,128]{5,4,3,2,1,0:T(8,128)S(1)} reduce(f32[4,2,2,32,2,16,128]{6,5,4,3,2,1,0:T(8,128)} %bitcast.53, f32[]{:T(128)} %constant.49.clone.1), dimensions={0}, to_apply=%region_1.2 | reduce | flops 1572864 | bytes 10485764 | tf_op jit(solution)/shard_map/reduce_sum | solution.py:98
  315.0 0.8 constant_dynamic-slice_fusion
  (10 shorter events, 0.1 us)
Async XLA Ops:
  7.2 7.5 %copy-start.2 = (f32[2,16,128]{2,1,0:T(8,128)S(1)}, f32[2,16,128]{2,1,0:T(8,128)}, u32[]{:S(2)}) copy-start(f32[2,16,128]{2,1,0:T(8,128)} %param.5) | copy-start | bytes 49156
  7.2 26.2 %copy-start.3 = (f32[2,16,128]{2,1,0:T(8,128)S(1)}, f32[2,16,128]{2,1,0:T(8,128)}, u32[]{:S(2)}) copy-start(f32[2,16,128]{2,1,0:T(8,128)} %param.6) | copy-start | bytes 49156
  7.2 34.5 %copy-start.4 = (f32[2,16,128]{2,1,0:T(8,128)S(1)}, f32[2,16,128]{2,1,0:T(8,128)}, u32[]{:S(2)}) copy-start(f32[2,16,128]{2,1,0:T(8,128)} %param.7) | copy-start | bytes 49156
  9.4 41.5 %all-to-all-start = ((f32[64,2,16,128]{3,2,1,0:T(8,128)}), f32[64,2,16,128]{3,2,1,0:T(8,128)S(1)}, u32[]{:S(2)}, u32[]{:S(2)}) async-start(f32[64,2,16,128]{3,2,1,0:T(8,128)} %bitcast), calls=%async_computation | async-start | bytes 2097152 | tf_op jit(solution)/shard_map/all_to_all | solution.py:59
  14.6 295.8 %all-gather.3.cloned.1.call-start = ((), (), s32[]{:S(2)}) async-start(), calls=%async_computation.2 | async-start | bytes 10485760 | tf_op jit(solution)/shard_map/all_gather | solution.py:98
  158.2 2.0 copy-start.1
  160.1 1.6 copy-start
Sparse Core Ops, SparseCore 0:
  160.3 150.0 all-gather.2
